TPU v7x, 256 devices: a whole 4x4x8 slice. The times are simulated.
256 devices in a mesh: slab: 16 (over x, z_lo, core), kern: 16 (over z_hi, y).
Axes of the slice: x: 4, y: 4, z: 8 (z_hi: 4, z_lo: 2; z = z_hi * 2 + z_lo), core: 2. Of those that a mesh axis runs over, the one named last changes fastest.
Arguments:
- mask_level: float32 [1024, 1024], P('slab'), may hold values from 0 to 1
- kernel_spectra: float32 [16, 2, 1024, 1024], P('kern', None, 'slab'), may hold values from -4.2 to 4.2
- socs_weight: float32 [16], replicated, may hold values from 0.05 to 0.5
- kernel_slot: int32 [16], replicated, may hold values from 0 to 15, each once
- blur_taps: float32 [31], replicated, may hold values from 0.005 to 0.06
- target: int32 [1024, 1024], P('slab'), may hold values 0 or 1
Outputs:
- mask_gradient: float32 [1024, 1024], P('slab', 'kern')
- resist_image: float32 [1024, 1024], P('slab', 'kern')
Inputs may be any that keep to these rules, and one draw needn't show every extreme that they name: `target`: every cell is 0 or 1. `kernel_slot`: each kernel number stands at exactly one slot.
All inputs are finite; a program needn't handle non-finite values. No bound on the sum of `target` on one device may be relied on, other than what follows from the above.
Results may differ from a plain program's by a relative error of at most 0.00017.
Values sent between devices are 32-bit elements; how exact they have to be, the bound alone decides.
A program may use at most 64 MiB of HBM per device.

v0:
```python
import math
import jax
import jax.numpy as jnp
from jax import lax
from jax.sharding import PartitionSpec as P

CQ = 128
STEEP = 4.0
LEVEL = 0.5


def swapped(shard, axis, apart):
    return lax.ppermute(shard, axis, [(i, i ^ 1 << apart) for i in range(lax.axis_size(axis))])


def padded_2(shard, sides, width):
    for axis, dim in sides:
        devices, length = (lax.axis_size(axis), shard.shape[dim])
        up = [(i, (i + 1) % devices) for i in range(devices - 1)]
        down = [(j, i) for i, j in up]
        last = lax.slice_in_dim(shard, length - width, length, axis=dim)
        initial = lax.slice_in_dim(shard, 0, width, axis=dim)
        before = lax.ppermute(last, axis, up)
        after = lax.ppermute(initial, axis, down)
        shard = jnp.concatenate([before, shard, after], axis=dim)
    return shard


def reversed_bits(number, num_bits):
    result = number * 0
    for bit_pos in range(num_bits):
        result = result * 2 + number // 2**bit_pos % 2
    return result


def rotation(product, length, sign_val):
    fraction = (product % length).astype(jnp.float32) / length
    angles = sign_val * 2.0 * math.pi * fraction
    return (jnp.cos(angles), jnp.sin(angles))


def complex_mul(first_pair, second_pair):
    real_part = first_pair[0] * second_pair[0] - first_pair[1] * second_pair[1]
    imag_part = first_pair[0] * second_pair[1] + first_pair[1] * second_pair[0]
    return (real_part, imag_part)


def table_product(pattern, matrix, values):
    highest = lax.Precision.HIGHEST

    def single(first_op, second_op):
        return jnp.einsum(pattern, first_op, second_op, precision=highest)

    if values[1] is None:
        return (single(matrix[0], values[0]), single(matrix[1], values[0]))
    real_part = single(matrix[0], values[0]) - single(matrix[1], values[1])
    imag_part = single(matrix[0], values[1]) + single(matrix[1], values[0])
    return (real_part, imag_part)


def columns_forward(values, outer_len, inner_len):
    extent = values[0].shape[0]
    shaped = tuple(
        (None if piece is None else piece.reshape(extent, outer_len, inner_len) for piece in values)
    )
    outer_idx = jnp.arange(outer_len)
    inner_idx = jnp.arange(inner_len)
    section = table_product(
        "ab,rbq->raq", rotation(outer_idx[:, None] * outer_idx[None, :], outer_len, -1.0), shaped
    )
    section = complex_mul(
        section, rotation(outer_idx[:, None] * inner_idx[None, :], outer_len * inner_len, -1.0)
    )
    return table_product(
        "bk,rpb->rpk", rotation(inner_idx[:, None] * inner_idx[None, :], inner_len, -1.0), section
    )


def columns_inverse(values, outer_len, inner_len, real_only):
    extent = values[0].shape[0]
    outer_idx = jnp.arange(outer_len)
    inner_idx = jnp.arange(inner_len)
    section = table_product(
        "bk,rpb->rpk", rotation(inner_idx[:, None] * inner_idx[None, :], inner_len, 1.0), values
    )
    section = complex_mul(
        section, rotation(outer_idx[:, None] * inner_idx[None, :], outer_len * inner_len, 1.0)
    )
    matrix = rotation(outer_idx[:, None] * outer_idx[None, :], outer_len, 1.0)
    if real_only:
        highest = lax.Precision.HIGHEST
        real_part = jnp.einsum("ab,rbq->raq", matrix[0], section[0], precision=highest)
        real_part = real_part - jnp.einsum("ab,rbq->raq", matrix[1], section[1], precision=highest)
        return real_part.reshape(extent, outer_len * inner_len)
    result = table_product("ab,rbq->raq", matrix, section)
    return (
        result[0].reshape(extent, outer_len * inner_len),
        result[1].reshape(extent, outer_len * inner_len),
    )


def rows_forward(values, freq_offset, full_width):
    extent = values[0].shape[0]
    positions = jnp.arange(extent)
    twiddle = rotation(positions * freq_offset, full_width, -1.0)
    values = complex_mul(values, (twiddle[0][:, None], twiddle[1][:, None]))
    return table_product(
        "sr,rc->sc", rotation(positions[:, None] * positions[None, :], extent, -1.0), values
    )


def rows_inverse(values, freq_offset, full_width):
    extent = values[0].shape[0]
    positions = jnp.arange(extent)
    values = table_product(
        "rs,sc->rc", rotation(positions[:, None] * positions[None, :], extent, 1.0), values
    )
    twiddle = rotation(positions * freq_offset, full_width, 1.0)
    return complex_mul(values, (twiddle[0][:, None], twiddle[1][:, None]))


def pairs_forward(stacked, num_bits):
    slab_index = lax.axis_index("slab")
    for bit_level in range(num_bits - 1, -1, -1):
        half_span = 2**bit_level
        partner = swapped(stacked, "slab", bit_level)
        is_upper = slab_index // half_span % 2 == 1
        twiddle = rotation(slab_index % half_span, 2 * half_span, -1.0)
        lower_val = stacked + partner
        difference = partner - stacked
        upper_val = jnp.stack(complex_mul((difference[0], difference[1]), twiddle))
        stacked = jnp.where(is_upper, upper_val, lower_val)
    return stacked


def pairs_inverse(stacked, num_bits):
    slab_index = lax.axis_index("slab")
    for bit_level in range(num_bits):
        half_span = 2**bit_level
        partner = swapped(stacked, "slab", bit_level)
        is_upper = slab_index // half_span % 2 == 1
        twiddle = rotation(slab_index % half_span, 2 * half_span, 1.0)
        from_upper = jnp.where(is_upper, stacked, partner)
        from_lower = jnp.where(is_upper, partner, stacked)
        turned = jnp.stack(complex_mul((from_upper[0], from_upper[1]), twiddle))
        stacked = jnp.where(is_upper, from_lower - turned, from_lower + turned)
    return stacked


def mix_forward(stacked, num_bits):
    return pairs_forward(stacked, num_bits)


def mix_inverse(stacked, num_bits):
    return pairs_inverse(stacked, num_bits)


def smooth(padded, kernel_taps, extent, span):
    tap_count = kernel_taps.shape[0]
    row_part = kernel_taps[0] * padded[0:extent, :]
    for tap_idx in range(1, tap_count):
        row_part = row_part + kernel_taps[tap_idx] * padded[tap_idx : tap_idx + extent, :]
    result = kernel_taps[0] * row_part[:, 0:span]
    for tap_idx in range(1, tap_count):
        result = result + kernel_taps[tap_idx] * row_part[:, tap_idx : tap_idx + span]
    return result


def resist_section(intensity_term, kernel_taps, target, kern_count, kern_index):
    reach = (kernel_taps.shape[0] - 1) // 2
    flipped = kernel_taps[::-1]
    extent, full_width = intensity_term.shape
    share_cols = full_width // kern_count

    def widen(values):
        padded = padded_2(values, (("slab", 0),), reach)
        return jnp.pad(padded, ((0, 0), (reach, reach)))

    summed = lax.psum(intensity_term, "kern")
    goal_cells = target.astype(jnp.float32)
    resist = jax.nn.sigmoid(
        STEEP * (smooth(widen(summed), kernel_taps, extent, full_width) - LEVEL)
    )
    slope_grad = 2.0 * (resist - goal_cells) * STEEP * resist * (1.0 - resist)
    cotangent = smooth(widen(slope_grad), flipped, extent, full_width)
    return (cotangent, lax.dynamic_slice_in_dim(resist, kern_index * share_cols, share_cols, 1))


def on_device(mask_level, kernel_spectra, socs_weight, kernel_slot, blur_taps, target):
    extent, full_width = mask_level.shape
    slab_count = lax.axis_size("slab")
    kern_count = lax.axis_size("kern")
    num_bits = slab_count.bit_length() - 1
    inner_len = CQ
    outer_len = full_width // inner_len
    freq_offset = reversed_bits(lax.axis_index("slab"), num_bits)
    kern_index = lax.axis_index("kern")
    kernel_id = jnp.sum(jnp.where(jnp.arange(kernel_slot.shape[0]) == kern_index, kernel_slot, 0))
    weight = jnp.sum(jnp.where(jnp.arange(socs_weight.shape[0]) == kernel_id, socs_weight, 0.0))
    arranged = kernel_spectra[0].reshape(2, extent, inner_len, outer_len).transpose(0, 1, 3, 2)
    transfer = (arranged[0], arranged[1])
    norm_scale = 1.0 / (full_width * full_width)

    def spectrum(values):
        columns = columns_forward(values, outer_len, inner_len)
        stacked = jnp.stack(columns).reshape(2, extent, full_width)
        stacked = mix_forward(stacked, num_bits)
        row_part = rows_forward((stacked[0], stacked[1]), freq_offset, full_width)
        return (
            row_part[0].reshape(extent, outer_len, inner_len),
            row_part[1].reshape(extent, outer_len, inner_len),
        )

    def back_to_cells(spectral, real_only):
        flat = (spectral[0].reshape(extent, full_width), spectral[1].reshape(extent, full_width))
        row_local = rows_inverse(flat, freq_offset, full_width)
        stacked = mix_inverse(jnp.stack(row_local), num_bits)
        shaped = (
            stacked[0].reshape(extent, outer_len, inner_len),
            stacked[1].reshape(extent, outer_len, inner_len),
        )
        return columns_inverse(shaped, outer_len, inner_len, real_only)

    mask_spec = spectrum((mask_level, None))
    field_val = back_to_cells(complex_mul(transfer, mask_spec), False)
    field_val = (field_val[0] * norm_scale, field_val[1] * norm_scale)
    intensity_term = weight * (field_val[0] * field_val[0] + field_val[1] * field_val[1])
    cotangent, resist = resist_section(intensity_term, blur_taps, target, kern_count, kern_index)
    factor = 2.0 * weight * cotangent
    carried_spec = spectrum((factor * field_val[0], factor * field_val[1]))
    gradient_term = (
        back_to_cells(complex_mul((transfer[0], -transfer[1]), carried_spec), True) * norm_scale
    )
    gradient = lax.psum_scatter(gradient_term, "kern", scatter_dimension=1, tiled=True)
    return (gradient, resist)


def solution(mesh):
    placed = (P("slab", None), P("kern", None, "slab", None), P(), P(), P(), P("slab", None))
    return jax.shard_map(
        on_device,
        mesh=mesh,
        in_specs=placed,
        out_specs=(P("slab", "kern"), P("slab", "kern")),
        check_vma=False,
    )
```

profile of v0, /device:TPU:2, one launch (start us, length us, event | category | flops | bytes accessed | tf_op | source)
XLA Modules:
  0.0 578.6 jit_solution(16228788483200270376)
XLA Ops:
  11.7 2.2 collective-permute-start
  14.1 12.9 %collective-permute-done = f32[2,64,1024]{2,1,0:T(8,128)S(1)} collective-permute-done((f32[2,64,1024]{2,1,0:T(8,128)S(1)}, f32[2,64,1024]{2,1,0:T(8,128)S(1)}, u32[]{:S(2)}, u32[]{:S(2)}) %collective-permute-start) | collective-permute-done | bytes 524320 | tf_op jit(solution)/shard_map/ppermute | solution.py:13
  27.8 12.3 %collective-permute-done.1 = f32[2,64,1024]{2,1,0:T(8,128)S(1)} collective-permute-done((f32[2,64,1024]{2,1,0:T(8,128)S(1)}, f32[2,64,1024]{2,1,0:T(8,128)S(1)}, u32[]{:S(2)}, u32[]{:S(2)}) %collective-permute-start.1) | collective-permute-done | bytes 524320 | tf_op jit(solution)/shard_map/ppermute | solution.py:13
  40.4 2.0 collective-permute-start.2
  42.6 10.0 %collective-permute-done.2 = f32[2,64,1024]{2,1,0:T(8,128)S(1)} collective-permute-done((f32[2,64,1024]{2,1,0:T(8,128)S(1)}, f32[2,64,1024]{2,1,0:T(8,128)S(1)}, u32[]{:S(2)}, u32[]{:S(2)}) %collective-permute-start.2) | collective-permute-done | bytes 524320 | tf_op jit(solution)/shard_map/ppermute | solution.py:13
  65.9 12.1 %collective-permute-done.5 = f32[2,64,1024]{2,1,0:T(8,128)S(1)} collective-permute-done((f32[2,64,1024]{2,1,0:T(8,128)S(1)}, f32[2,64,1024]{2,1,0:T(8,128)S(1)}, u32[]{:S(2)}, u32[]{:S(2)}) %collective-permute-start.5) | collective-permute-done | bytes 524320 | tf_op jit(solution)/shard_map/ppermute | solution.py:13
  79.3 12.4 %collective-permute-done.6 = f32[2,64,1024]{2,1,0:T(8,128)S(1)} collective-permute-done((f32[2,64,1024]{2,1,0:T(8,128)S(1)}, f32[2,64,1024]{2,1,0:T(8,128)S(1)}, u32[]{:S(2)}, u32[]{:S(2)}) %collective-permute-start.6) | collective-permute-done | bytes 524320 | tf_op jit(solution)/shard_map/ppermute | solution.py:13
  92.0 2.2 collective-permute-start.7
  97.0 8.9 %collective-permute-done.7 = f32[2,64,1024]{2,1,0:T(8,128)S(1)} collective-permute-done((f32[2,64,1024]{2,1,0:T(8,128)S(1)}, f32[2,64,1024]{2,1,0:T(8,128)S(1)}, u32[]{:S(2)}, u32[]{:S(2)}) %collective-permute-start.7) | collective-permute-done | bytes 524320 | tf_op jit(solution)/shard_map/ppermute | solution.py:13
  113.2 167.5 %all-reduce.4.cloned.1.call-done = f32[64,1024]{1,0:T(8,128)} async-done(((f32[64,1024]{1,0:T(8,128)}), f32[64,1024]{1,0:T(8,128)}) %all-reduce.4.cloned.1.call-update) | async-done | bytes 262160 | tf_op jit(solution)/shard_map/psum | solution.py:179
  283.6 4.5 collective-permute-start.9
  290.2 20.0 %fusion.37 = f32[64,1054]{1,0:T(8,128)S(1)} fusion(f32[94,1054]{1,0:T(8,128)S(1)} %select_maximum_fusion.2, f32[]{:T(128)} %bitcast.49, f32[]{:T(128)} %bitcast.48, f32[]{:T(128)} %bitcast.47, f32[]{:T(128)} %bitcast.46, f32[]{:T(128)} %bitcast.45, f32[]{:T(128)} %bitcast.44, f32[]{:T(128)} %bitcast.43, f32[]{:T(128)} %bitcast.42, f32[]{:T(128)} %bitcast.41, ...), kind=kLoop, calls=%fused_computation.122 | loop fusion | flops 4114816 | bytes 8634492 | tf_op jit(solution)/shard_map/add | solution.py:162
  310.3 21.3 %subtract_multiply_fusion = (f32[64,1024]{1,0:T(8,128)S(1)}, f32[64,1024]{1,0:T(8,128)S(1)}) fusion(s32[64,1024]{1,0:T(8,128)S(1)} %copy-done.3, f32[64,1054]{1,0:T(8,128)S(1)} %fusion.37, f32[]{:T(128)} %bitcast.2, f32[]{:T(128)} %bitcast.49, f32[]{:T(128)} %bitcast.48, f32[]{:T(128)} %bitcast.47, f32[]{:T(128)} %bitcast.46, f32[]{:T(128)} %bitcast.45, ...), kind=kLoop, calls=%fused_computation.373 | loop fusion | flops 4718592 | bytes 8913020 | tf_op jit(solution)/shard_map/mul | solution.py:184
  333.5 4.8 collective-permute-start.11
  340.2 20.0 %fusion.7 = f32[64,1054]{1,0:T(8,128)S(1)} fusion(f32[94,1054]{1,0:T(8,128)S(1)} %select_maximum_fusion, f32[]{:T(128)} %bitcast.49, f32[]{:T(128)} %bitcast.48, f32[]{:T(128)} %bitcast.47, f32[]{:T(128)} %bitcast.46, f32[]{:T(128)} %bitcast.45, f32[]{:T(128)} %bitcast.44, f32[]{:T(128)} %bitcast.43, f32[]{:T(128)} %bitcast.42, f32[]{:T(128)} %bitcast.41, ...), kind=kLoop, calls=%fused_computation.61 | loop fusion | flops 4114816 | bytes 8634492 | tf_op jit(solution)/shard_map/add | solution.py:162
  360.2 21.3 %fusion.70 = (f32[8,8,8,128]{3,1,2,0:T(8,128)S(1)}, f32[64,1024]{1,0:T(8,128)S(1)}) fusion(f32[8,8,8,128]{3,2,1,0:T(8,128)S(1)} %bitcast.291, f32[64,1054]{1,0:T(8,128)S(1)} %fusion.7, f32[]{:T(128)} %bitcast.3, f32[]{:T(128)} %bitcast.21, f32[]{:T(128)} %bitcast.22, f32[]{:T(128)} %bitcast.23, f32[]{:T(128)} %bitcast.24, f32[]{:T(128)} %bitcast.25, ...), kind=kLoop, calls=%fused_computation.189 | loop fusion | flops 4128768 | bytes 8913024
  386.0 2.2 collective-permute-start.12
  388.2 13.8 %collective-permute-done.12 = f32[2,64,1024]{2,1,0:T(8,128)S(1)} collective-permute-done((f32[2,64,1024]{2,1,0:T(8,128)S(1)}, f32[2,64,1024]{2,1,0:T(8,128)S(1)}, u32[]{:S(2)}, u32[]{:S(2)}) %collective-permute-start.12) | collective-permute-done | bytes 524320 | tf_op jit(solution)/shard_map/ppermute | solution.py:13
  402.6 13.2 %collective-permute-done.13 = f32[2,64,1024]{2,1,0:T(8,128)S(1)} collective-permute-done((f32[2,64,1024]{2,1,0:T(8,128)S(1)}, f32[2,64,1024]{2,1,0:T(8,128)S(1)}, u32[]{:S(2)}, u32[]{:S(2)}) %collective-permute-start.13) | collective-permute-done | bytes 524320 | tf_op jit(solution)/shard_map/ppermute | solution.py:13
  416.2 12.7 %collective-permute-done.14 = f32[2,64,1024]{2,1,0:T(8,128)S(1)} collective-permute-done((f32[2,64,1024]{2,1,0:T(8,128)S(1)}, f32[2,64,1024]{2,1,0:T(8,128)S(1)}, u32[]{:S(2)}, u32[]{:S(2)}) %collective-permute-start.14) | collective-permute-done | bytes 524320 | tf_op jit(solution)/shard_map/ppermute | solution.py:13
  439.6 12.6 %collective-permute-done.17 = f32[2,64,1024]{2,1,0:T(8,128)S(1)} collective-permute-done((f32[2,64,1024]{2,1,0:T(8,128)S(1)}, f32[2,64,1024]{2,1,0:T(8,128)S(1)}, u32[]{:S(2)}, u32[]{:S(2)}) %collective-permute-start.17) | collective-permute-done | bytes 524320 | tf_op jit(solution)/shard_map/ppermute | solution.py:13
  454.0 11.9 %collective-permute-done.18 = f32[2,64,1024]{2,1,0:T(8,128)S(1)} collective-permute-done((f32[2,64,1024]{2,1,0:T(8,128)S(1)}, f32[2,64,1024]{2,1,0:T(8,128)S(1)}, u32[]{:S(2)}, u32[]{:S(2)}) %collective-permute-start.18) | collective-permute-done | bytes 524320 | tf_op jit(solution)/shard_map/ppermute | solution.py:13
  466.9 13.2 %collective-permute-done.19 = f32[2,64,1024]{2,1,0:T(8,128)S(1)} collective-permute-done((f32[2,64,1024]{2,1,0:T(8,128)S(1)}, f32[2,64,1024]{2,1,0:T(8,128)S(1)}, u32[]{:S(2)}, u32[]{:S(2)}) %collective-permute-start.19) | collective-permute-done | bytes 524320 | tf_op jit(solution)/shard_map/ppermute | solution.py:13
  485.6 84.6 %reduce-scatter.4.cloned.1.call-done = f32[64,64]{1,0:T(8,128)} async-done(((f32[1024,64]{1,0:T(8,128)}), f32[64,64]{1,0:T(8,128)}) %reduce-scatter.4.cloned.1.call-update) | async-done | bytes 16400
  (170 shorter events, 63.0 us)
Async XLA Ops:
  7.2 273.5 %all-reduce.4.cloned.1.call-start = ((), (), s32[]{:S(2)}) async-start(), calls=%async_computation.1 | async-start | bytes 524288 | tf_op jit(solution)/shard_map/psum | solution.py:179
  11.7 15.3 %collective-permute-start = (f32[2,64,1024]{2,1,0:T(8,128)S(1)}, f32[2,64,1024]{2,1,0:T(8,128)S(1)}, u32[]{:S(2)}, u32[]{:S(2)}) collective-permute-start(f32[2,64,1024]{2,1,0:T(8,128)S(1)} %constant_dynamic-update-slice_fusion), channel_id=1, source_target_pairs={{0,128},{16,144},{32,160},{48,176},{64,192},{80,208},{96,224},{112... | collective-permute-start | bytes 1572872 | tf_op jit(solution)/shard_map/ppermute | solution.py:13
  27.2 12.9 %collective-permute-start.1 = (f32[2,64,1024]{2,1,0:T(8,128)S(1)}, f32[2,64,1024]{2,1,0:T(8,128)S(1)}, u32[]{:S(2)}, u32[]{:S(2)}) collective-permute-start(f32[2,64,1024]{2,1,0:T(8,128)S(1)} %maximum_select_fusion), channel_id=1, source_target_pairs={{0,64},{16,80},{32,96},{48,112},{64,0},{80,16},{96,32},{112,48},{1... | collective-permute-start | bytes 1572872 | tf_op jit(solution)/shard_map/ppermute | solution.py:13
  40.4 12.2 %collective-permute-start.2 = (f32[2,64,1024]{2,1,0:T(8,128)S(1)}, f32[2,64,1024]{2,1,0:T(8,128)S(1)}, u32[]{:S(2)}, u32[]{:S(2)}) collective-permute-start(f32[2,64,1024]{2,1,0:T(8,128)S(1)} %maximum_select_fusion.1), channel_id=1, source_target_pairs={{0,32},{16,48},{32,0},{48,16},{64,96},{80,112},{96,64},{112,80},{1... | collective-permute-start | bytes 1572872 | tf_op jit(solution)/shard_map/ppermute | solution.py:13
  52.8 3.7 collective-permute-start.3
  61.2 2.5 collective-permute-start.4
  63.9 14.1 %collective-permute-start.5 = (f32[2,64,1024]{2,1,0:T(8,128)S(1)}, f32[2,64,1024]{2,1,0:T(8,128)S(1)}, u32[]{:S(2)}, u32[]{:S(2)}) collective-permute-start(f32[2,64,1024]{2,1,0:T(8,128)S(1)} %add_select_fusion.7), channel_id=1, source_target_pairs={{0,32},{16,48},{32,0},{48,16},{64,96},{80,112},{96,64},{112,80},{1... | collective-permute-start | bytes 1572872 | tf_op jit(solution)/shard_map/ppermute | solution.py:13
  78.5 13.2 %collective-permute-start.6 = (f32[2,64,1024]{2,1,0:T(8,128)S(1)}, f32[2,64,1024]{2,1,0:T(8,128)S(1)}, u32[]{:S(2)}, u32[]{:S(2)}) collective-permute-start(f32[2,64,1024]{2,1,0:T(8,128)S(1)} %add_select_fusion.6), channel_id=1, source_target_pairs={{0,64},{16,80},{32,96},{48,112},{64,0},{80,16},{96,32},{112,48},{1... | collective-permute-start | bytes 1572872 | tf_op jit(solution)/shard_map/ppermute | solution.py:13
  92.0 13.9 %collective-permute-start.7 = (f32[2,64,1024]{2,1,0:T(8,128)S(1)}, f32[2,64,1024]{2,1,0:T(8,128)S(1)}, u32[]{:S(2)}, u32[]{:S(2)}) collective-permute-start(f32[2,64,1024]{2,1,0:T(8,128)S(1)} %add_select_fusion.5), channel_id=1, source_target_pairs={{0,128},{16,144},{32,160},{48,176},{64,192},{80,208},{96,224},{112... | collective-permute-start | bytes 1572872 | tf_op jit(solution)/shard_map/ppermute | solution.py:13
  111.9 458.3 %reduce-scatter.4.cloned.1.call-start = ((), (), s32[]{:S(2)}) async-start(), calls=%async_computation.2 | async-start | bytes 557056
  280.7 9.3 %copy-start = (f32[64,1024]{1,0:T(8,128)S(1)}, f32[64,1024]{1,0:T(8,128)}, u32[]{:S(2)}) copy-start(f32[64,1024]{1,0:T(8,128)} %all-reduce.4.cloned.1.call-done) | copy-start | bytes 786436
  281.6 7.2 %collective-permute-start.8 = (f32[15,1024]{1,0:T(8,128)S(1)}, f32[15,1024]{1,0:T(8,128)S(1)}, u32[]{:S(2)}, u32[]{:S(2)}) collective-permute-start(f32[15,1024]{1,0:T(8,128)S(1)} %get-tuple-element.54), channel_id=1, source_target_pairs={{0,16},{16,32},{32,48},{48,64},{64,80},{80,96},{96,112},{112,128},... | collective-permute-start | bytes 184328 | tf_op jit(solution)/shard_map/ppermute | solution.py:23
  283.6 6.4 %collective-permute-start.9 = (f32[15,1024]{1,0:T(8,128)S(1)}, f32[15,1024]{1,0:T(8,128)S(1)}, u32[]{:S(2)}, u32[]{:S(2)}) collective-permute-start(f32[15,1024]{1,0:T(8,128)S(1)} %get-tuple-element.55), channel_id=1, source_target_pairs={{16,0},{32,16},{48,32},{64,48},{80,64},{96,80},{112,96},{128,112},... | collective-permute-start | bytes 184328 | tf_op jit(solution)/shard_map/ppermute | solution.py:24
  290.2 20.1 %copy-start.3 = (s32[64,1024]{1,0:T(8,128)S(1)}, s32[64,1024]{1,0:T(8,128)}, u32[]{:S(2)}) copy-start(s32[64,1024]{1,0:T(8,128)} %param.11) | copy-start | bytes 786436
  331.6 7.4 %collective-permute-start.10 = (f32[15,1024]{1,0:T(8,128)S(1)}, f32[15,1024]{1,0:T(8,128)S(1)}, u32[]{:S(2)}, u32[]{:S(2)}) collective-permute-start(f32[15,1024]{1,0:T(8,128)S(1)} %get-tuple-element.52), channel_id=1, source_target_pairs={{0,16},{16,32},{32,48},{48,64},{64,80},{80,96},{96,112},{112,128},... | collective-permute-start | bytes 184328 | tf_op jit(solution)/shard_map/ppermute | solution.py:23
  333.5 6.5 %collective-permute-start.11 = (f32[15,1024]{1,0:T(8,128)S(1)}, f32[15,1024]{1,0:T(8,128)S(1)}, u32[]{:S(2)}, u32[]{:S(2)}) collective-permute-start(f32[15,1024]{1,0:T(8,128)S(1)} %get-tuple-element.53), channel_id=1, source_target_pairs={{16,0},{32,16},{48,32},{64,48},{80,64},{96,80},{112,96},{128,112},... | collective-permute-start | bytes 184328 | tf_op jit(solution)/shard_map/ppermute | solution.py:24
  386.0 16.0 %collective-permute-start.12 = (f32[2,64,1024]{2,1,0:T(8,128)S(1)}, f32[2,64,1024]{2,1,0:T(8,128)S(1)}, u32[]{:S(2)}, u32[]{:S(2)}) collective-permute-start(f32[2,64,1024]{2,1,0:T(8,128)S(1)} %constant_dynamic-update-slice_fusion.2), channel_id=1, source_target_pairs={{0,128},{16,144},{32,160},{48,176},{64,192},{80,208},{96,224},{112... | collective-permute-start | bytes 1572872 | tf_op jit(solution)/shard_map/ppermute | solution.py:13
  402.2 13.6 %collective-permute-start.13 = (f32[2,64,1024]{2,1,0:T(8,128)S(1)}, f32[2,64,1024]{2,1,0:T(8,128)S(1)}, u32[]{:S(2)}, u32[]{:S(2)}) collective-permute-start(f32[2,64,1024]{2,1,0:T(8,128)S(1)} %maximum_select_fusion.4), channel_id=1, source_target_pairs={{0,64},{16,80},{32,96},{48,112},{64,0},{80,16},{96,32},{112,48},{1... | collective-permute-start | bytes 1572872 | tf_op jit(solution)/shard_map/ppermute | solution.py:13
  416.1 12.8 %collective-permute-start.14 = (f32[2,64,1024]{2,1,0:T(8,128)S(1)}, f32[2,64,1024]{2,1,0:T(8,128)S(1)}, u32[]{:S(2)}, u32[]{:S(2)}) collective-permute-start(f32[2,64,1024]{2,1,0:T(8,128)S(1)} %maximum_select_fusion.5), channel_id=1, source_target_pairs={{0,32},{16,48},{32,0},{48,16},{64,96},{80,112},{96,64},{112,80},{1... | collective-permute-start | bytes 1572872 | tf_op jit(solution)/shard_map/ppermute | solution.py:13
  429.1 2.2 collective-permute-start.15
  435.9 2.0 collective-permute-start.16
  438.2 14.1 %collective-permute-start.17 = (f32[2,64,1024]{2,1,0:T(8,128)S(1)}, f32[2,64,1024]{2,1,0:T(8,128)S(1)}, u32[]{:S(2)}, u32[]{:S(2)}) collective-permute-start(f32[2,64,1024]{2,1,0:T(8,128)S(1)} %add_select_fusion.3), channel_id=1, source_target_pairs={{0,32},{16,48},{32,0},{48,16},{64,96},{80,112},{96,64},{112,80},{1... | collective-permute-start | bytes 1572872 | tf_op jit(solution)/shard_map/ppermute | solution.py:13
  452.8 13.2 %collective-permute-start.18 = (f32[2,64,1024]{2,1,0:T(8,128)S(1)}, f32[2,64,1024]{2,1,0:T(8,128)S(1)}, u32[]{:S(2)}, u32[]{:S(2)}) collective-permute-start(f32[2,64,1024]{2,1,0:T(8,128)S(1)} %add_select_fusion.2), channel_id=1, source_target_pairs={{0,64},{16,80},{32,96},{48,112},{64,0},{80,16},{96,32},{112,48},{1... | collective-permute-start | bytes 1572872 | tf_op jit(solution)/shard_map/ppermute | solution.py:13
  466.2 13.8 %collective-permute-start.19 = (f32[2,64,1024]{2,1,0:T(8,128)S(1)}, f32[2,64,1024]{2,1,0:T(8,128)S(1)}, u32[]{:S(2)}, u32[]{:S(2)}) collective-permute-start(f32[2,64,1024]{2,1,0:T(8,128)S(1)} %add_select_fusion.1), channel_id=1, source_target_pairs={{0,128},{16,144},{32,160},{48,176},{64,192},{80,208},{96,224},{112... | collective-permute-start | bytes 1572872 | tf_op jit(solution)/shard_map/ppermute | solution.py:13
  (4 other events, 3.0 us)
Sparse Core Ops, SparseCore 0:
  112.0 168.6 all-reduce.3
  485.0 85.1 reduce-scatter.3
where the time goes:
time: 588 us; the launch traced here: 579 us
  waiting for transfers between devices  406 us (69%)
  other arithmetic  90.9 us (15%)
  starting transfers between devices  29.8 us (5%)
  matrix products  23.2 us (4%)
  between operations  17 us (3%)
  local copies, waits for them, and re-layouts  11.9 us (2%)
    psum x1, waiting for transfers between devices, resist_section(): summed = lax.psum(intensity_term, 'kern')  168 us
    ppermute x16, waiting for transfers between devices, swapped(): lax.ppermute(shard, axis, [(i, i ^ 1 << apart) for i in range(lax.axis_si...  152 us
    unnamed x3, waiting for transfers between devices  84.6 us
    add x2, other arithmetic, smooth(): row_part + kernel_taps[tap_idx] * padded[tap_idx:tap_idx + extent, :]  40 us
    dot_general x42, matrix products, single(): return jnp.einsum(pattern, first_op, second_op, precision=highest)  22.4 us
    unnamed x2, other arithmetic  21.4 us
    mul x1, other arithmetic, resist_section(): slope_grad = 2.0 * (resist - goal_cells) * STEEP * resist * (1.0 - resist)  21.3 us
    ppermute x16, starting transfers between devices, swapped(): lax.ppermute(shard, axis, [(i, i ^ 1 << apart) for i in range(lax.axis_si...  16.5 us
  transfers between devices with their start and end apart: 22, of which 19 were waited for; matrix products, arithmetic and copies ran while one was open for 1% of the time, Pallas kernels for 0%

commit v1 on v0

--- a/solution.py
+++ b/solution.py
@@ -1,3 +1,4 @@
+import functools
 import math
 import jax
 import jax.numpy as jnp
@@ -7,6 +8,14 @@
 CQ = 128
 STEEP = 4.0
 LEVEL = 0.5
+
+
+def report_row(m, row_axis):
+    h_now = lax.all_gather(m, row_axis)
+    return jnp.sum(h_now, 0)
+
+
+read_task_now = functools.partial(report_row, row_axis="kern")
 
 
 def swapped(shard, axis, apart):
@@ -176,7 +185,7 @@
         padded = padded_2(values, (("slab", 0),), reach)
         return jnp.pad(padded, ((0, 0), (reach, reach)))
 
-    summed = lax.psum(intensity_term, "kern")
+    summed = read_task_now(intensity_term)
     goal_cells = target.astype(jnp.float32)
     resist = jax.nn.sigmoid(
         STEEP * (smooth(widen(summed), kernel_taps, extent, full_width) - LEVEL)

time: 588 us -> 502 us (0.85)
  waiting for transfers between devices: 406 us -> 315 us
    psum x1 -> x0, waiting for transfers between devices: 168 us -> none  [resist_section(): summed = lax.psum(intensity_term, 'kern')]
    all_gather x0 -> x1, waiting for transfers between devices: none -> 77.1 us  [report_row(): h_now = lax.all_gather(m, row_axis)]
where the time goes in v1:
time: 502 us; the launch traced here: 492 us
  waiting for transfers between devices  315 us (63%)
  other arithmetic  93.2 us (19%)
  starting transfers between devices  33.6 us (7%)
  matrix products  23.2 us (5%)
  between operations  17.1 us (3%)
  local copies, waits for them, and re-layouts  9.74 us (2%)
    ppermute x16, waiting for transfers between devices, swapped(): lax.ppermute(shard, axis, [(i, i ^ 1 << apart) for i in range(lax.axis_si...  151 us
    unnamed x3, waiting for transfers between devices  85.5 us
    all_gather x1, waiting for transfers between devices, report_row(): h_now = lax.all_gather(m, row_axis)  77.1 us
    add x2, other arithmetic, smooth(): row_part + kernel_taps[tap_idx] * padded[tap_idx:tap_idx + extent, :]  40.3 us
    dot_general x42, matrix products, single(): return jnp.einsum(pattern, first_op, second_op, precision=highest)  22.4 us
    unnamed x2, other arithmetic  21.5 us
    mul x1, other arithmetic, resist_section(): slope_grad = 2.0 * (resist - goal_cells) * STEEP * resist * (1.0 - resist)  21.5 us
    ppermute x16, starting transfers between devices, swapped(): lax.ppermute(shard, axis, [(i, i ^ 1 << apart) for i in range(lax.axis_si...  20.2 us
  transfers between devices with their start and end apart: 22, of which 19 were waited for; matrix products, arithmetic and copies ran while one was open for 1% of the time, Pallas kernels for 0%

profile of v1, /device:TPU:2, one launch (start us, length us, event | category | flops | bytes accessed | tf_op | source)
XLA Modules:
  0.0 492.3 jit_solution(7041798640544459344)
XLA Ops:
  14.1 12.9 %collective-permute-done = f32[2,64,1024]{2,1,0:T(8,128)S(1)} collective-permute-done((f32[2,64,1024]{2,1,0:T(8,128)S(1)}, f32[2,64,1024]{2,1,0:T(8,128)S(1)}, u32[]{:S(2)}, u32[]{:S(2)}) %collective-permute-start) | collective-permute-done | bytes 524320 | tf_op jit(solution)/shard_map/ppermute | solution.py:22
  27.8 12.3 %collective-permute-done.1 = f32[2,64,1024]{2,1,0:T(8,128)S(1)} collective-permute-done((f32[2,64,1024]{2,1,0:T(8,128)S(1)}, f32[2,64,1024]{2,1,0:T(8,128)S(1)}, u32[]{:S(2)}, u32[]{:S(2)}) %collective-permute-start.1) | collective-permute-done | bytes 524320 | tf_op jit(solution)/shard_map/ppermute | solution.py:22
  42.6 10.0 %collective-permute-done.2 = f32[2,64,1024]{2,1,0:T(8,128)S(1)} collective-permute-done((f32[2,64,1024]{2,1,0:T(8,128)S(1)}, f32[2,64,1024]{2,1,0:T(8,128)S(1)}, u32[]{:S(2)}, u32[]{:S(2)}) %collective-permute-start.2) | collective-permute-done | bytes 524320 | tf_op jit(solution)/shard_map/ppermute | solution.py:22
  65.2 12.3 %collective-permute-done.5 = f32[2,64,1024]{2,1,0:T(8,128)S(1)} collective-permute-done((f32[2,64,1024]{2,1,0:T(8,128)S(1)}, f32[2,64,1024]{2,1,0:T(8,128)S(1)}, u32[]{:S(2)}, u32[]{:S(2)}) %collective-permute-start.5) | collective-permute-done | bytes 524320 | tf_op jit(solution)/shard_map/ppermute | solution.py:22
  78.9 12.6 %collective-permute-done.6 = f32[2,64,1024]{2,1,0:T(8,128)S(1)} collective-permute-done((f32[2,64,1024]{2,1,0:T(8,128)S(1)}, f32[2,64,1024]{2,1,0:T(8,128)S(1)}, u32[]{:S(2)}, u32[]{:S(2)}) %collective-permute-start.6) | collective-permute-done | bytes 524320 | tf_op jit(solution)/shard_map/ppermute | solution.py:22
  96.1 9.8 %collective-permute-done.7 = f32[2,64,1024]{2,1,0:T(8,128)S(1)} collective-permute-done((f32[2,64,1024]{2,1,0:T(8,128)S(1)}, f32[2,64,1024]{2,1,0:T(8,128)S(1)}, u32[]{:S(2)}, u32[]{:S(2)}) %collective-permute-start.7) | collective-permute-done | bytes 524320 | tf_op jit(solution)/shard_map/ppermute | solution.py:22
  112.7 77.1 %all-gather.2.cloned.1.call-done = f32[16,64,1024]{2,1,0:T(8,128)} async-done(((f32[1,64,1024]{2,1,0:T(8,128)}), f32[16,64,1024]{2,1,0:T(8,128)}) %all-gather.2.cloned.1.call-update) | async-done | bytes 4194320 | tf_op jit(solution)/shard_map/all_gather | solution.py:14
  189.8 2.5 reduce_sum.29
  194.3 4.7 collective-permute-start.9
  201.1 20.2 %fusion.37 = f32[64,1054]{1,0:T(8,128)S(1)} fusion(f32[94,1054]{1,0:T(8,128)S(1)} %select_maximum_fusion.2, f32[]{:T(128)} %bitcast.48, f32[]{:T(128)} %bitcast.47, f32[]{:T(128)} %bitcast.46, f32[]{:T(128)} %bitcast.45, f32[]{:T(128)} %bitcast.44, f32[]{:T(128)} %bitcast.43, f32[]{:T(128)} %bitcast.42, f32[]{:T(128)} %bitcast.41, f32[]{:T(128)} %bitcast.40, ...), kind=kLoop, calls=%fused_computation.122 | loop fusion | flops 4114816 | bytes 8634492 | tf_op jit(solution)/shard_map/add | solution.py:171
  221.3 21.5 %subtract_multiply_fusion = (f32[64,1024]{1,0:T(8,128)S(1)}, f32[64,1024]{1,0:T(8,128)S(1)}) fusion(s32[64,1024]{1,0:T(8,128)S(1)} %copy-done.2, f32[64,1054]{1,0:T(8,128)S(1)} %fusion.37, f32[]{:T(128)} %bitcast.2, f32[]{:T(128)} %bitcast.48, f32[]{:T(128)} %bitcast.47, f32[]{:T(128)} %bitcast.46, f32[]{:T(128)} %bitcast.45, f32[]{:T(128)} %bitcast.44, ...), kind=kLoop, calls=%fused_computation.370 | loop fusion | flops 4718592 | bytes 8913020 | tf_op jit(solution)/shard_map/mul | solution.py:193
  242.8 4.4 collective-permute-start.10
  247.2 2.2 collective-permute-start.11
  251.4 20.1 %fusion.7 = f32[64,1054]{1,0:T(8,128)S(1)} fusion(f32[94,1054]{1,0:T(8,128)S(1)} %select_maximum_fusion, f32[]{:T(128)} %bitcast.48, f32[]{:T(128)} %bitcast.47, f32[]{:T(128)} %bitcast.46, f32[]{:T(128)} %bitcast.45, f32[]{:T(128)} %bitcast.44, f32[]{:T(128)} %bitcast.43, f32[]{:T(128)} %bitcast.42, f32[]{:T(128)} %bitcast.41, f32[]{:T(128)} %bitcast.40, ...), kind=kLoop, calls=%fused_computation.61 | loop fusion | flops 4114816 | bytes 8634492 | tf_op jit(solution)/shard_map/add | solution.py:171
  271.5 21.4 %fusion.68 = (f32[8,8,8,128]{3,1,2,0:T(8,128)S(1)}, f32[64,1024]{1,0:T(8,128)S(1)}) fusion(f32[8,8,8,128]{3,2,1,0:T(8,128)S(1)} %bitcast.283, f32[64,1054]{1,0:T(8,128)S(1)} %fusion.7, f32[]{:T(128)} %bitcast.3, f32[]{:T(128)} %bitcast.20, f32[]{:T(128)} %bitcast.21, f32[]{:T(128)} %bitcast.22, f32[]{:T(128)} %bitcast.23, f32[]{:T(128)} %bitcast.24, ...), kind=kLoop, calls=%fused_computation.185 | loop fusion | flops 4128768 | bytes 8913024
  297.4 2.7 collective-permute-start.12
  300.1 13.0 %collective-permute-done.12 = f32[2,64,1024]{2,1,0:T(8,128)S(1)} collective-permute-done((f32[2,64,1024]{2,1,0:T(8,128)S(1)}, f32[2,64,1024]{2,1,0:T(8,128)S(1)}, u32[]{:S(2)}, u32[]{:S(2)}) %collective-permute-start.12) | collective-permute-done | bytes 524320 | tf_op jit(solution)/shard_map/ppermute | solution.py:22
  313.7 14.1 %collective-permute-done.13 = f32[2,64,1024]{2,1,0:T(8,128)S(1)} collective-permute-done((f32[2,64,1024]{2,1,0:T(8,128)S(1)}, f32[2,64,1024]{2,1,0:T(8,128)S(1)}, u32[]{:S(2)}, u32[]{:S(2)}) %collective-permute-start.13) | collective-permute-done | bytes 524320 | tf_op jit(solution)/shard_map/ppermute | solution.py:22
  329.6 12.0 %collective-permute-done.14 = f32[2,64,1024]{2,1,0:T(8,128)S(1)} collective-permute-done((f32[2,64,1024]{2,1,0:T(8,128)S(1)}, f32[2,64,1024]{2,1,0:T(8,128)S(1)}, u32[]{:S(2)}, u32[]{:S(2)}) %collective-permute-start.14) | collective-permute-done | bytes 524320 | tf_op jit(solution)/shard_map/ppermute | solution.py:22
  352.7 12.3 %collective-permute-done.17 = f32[2,64,1024]{2,1,0:T(8,128)S(1)} collective-permute-done((f32[2,64,1024]{2,1,0:T(8,128)S(1)}, f32[2,64,1024]{2,1,0:T(8,128)S(1)}, u32[]{:S(2)}, u32[]{:S(2)}) %collective-permute-start.17) | collective-permute-done | bytes 524320 | tf_op jit(solution)/shard_map/ppermute | solution.py:22
  366.0 12.7 %collective-permute-done.18 = f32[2,64,1024]{2,1,0:T(8,128)S(1)} collective-permute-done((f32[2,64,1024]{2,1,0:T(8,128)S(1)}, f32[2,64,1024]{2,1,0:T(8,128)S(1)}, u32[]{:S(2)}, u32[]{:S(2)}) %collective-permute-start.18) | collective-permute-done | bytes 524320 | tf_op jit(solution)/shard_map/ppermute | solution.py:22
  379.0 2.5 collective-permute-start.19
  381.5 11.4 %collective-permute-done.19 = f32[2,64,1024]{2,1,0:T(8,128)S(1)} collective-permute-done((f32[2,64,1024]{2,1,0:T(8,128)S(1)}, f32[2,64,1024]{2,1,0:T(8,128)S(1)}, u32[]{:S(2)}, u32[]{:S(2)}) %collective-permute-start.19) | collective-permute-done | bytes 524320 | tf_op jit(solution)/shard_map/ppermute | solution.py:22
  398.3 85.5 %reduce-scatter.4.cloned.1.call-done = f32[64,64]{1,0:T(8,128)} async-done(((f32[1024,64]{1,0:T(8,128)}), f32[64,64]{1,0:T(8,128)}) %reduce-scatter.4.cloned.1.call-update) | async-done | bytes 16400
  (170 shorter events, 65.0 us)
Async XLA Ops:
  7.2 182.7 %all-gather.2.cloned.1.call-start = ((), (), s32[]{:S(2)}) async-start(), calls=%async_computation.1 | async-start | bytes 4456448 | tf_op jit(solution)/shard_map/all_gather | solution.py:14
  11.7 15.3 %collective-permute-start = (f32[2,64,1024]{2,1,0:T(8,128)S(1)}, f32[2,64,1024]{2,1,0:T(8,128)S(1)}, u32[]{:S(2)}, u32[]{:S(2)}) collective-permute-start(f32[2,64,1024]{2,1,0:T(8,128)S(1)} %constant_dynamic-update-slice_fusion), channel_id=1, source_target_pairs={{0,128},{16,144},{32,160},{48,176},{64,192},{80,208},{96,224},{112... | collective-permute-start | bytes 1572872 | tf_op jit(solution)/shard_map/ppermute | solution.py:22
  27.2 12.9 %collective-permute-start.1 = (f32[2,64,1024]{2,1,0:T(8,128)S(1)}, f32[2,64,1024]{2,1,0:T(8,128)S(1)}, u32[]{:S(2)}, u32[]{:S(2)}) collective-permute-start(f32[2,64,1024]{2,1,0:T(8,128)S(1)} %maximum_select_fusion), channel_id=1, source_target_pairs={{0,64},{16,80},{32,96},{48,112},{64,0},{80,16},{96,32},{112,48},{1... | collective-permute-start | bytes 1572872 | tf_op jit(solution)/shard_map/ppermute | solution.py:22
  40.4 12.2 %collective-permute-start.2 = (f32[2,64,1024]{2,1,0:T(8,128)S(1)}, f32[2,64,1024]{2,1,0:T(8,128)S(1)}, u32[]{:S(2)}, u32[]{:S(2)}) collective-permute-start(f32[2,64,1024]{2,1,0:T(8,128)S(1)} %maximum_select_fusion.1), channel_id=1, source_target_pairs={{0,32},{16,48},{32,0},{48,16},{64,96},{80,112},{96,64},{112,80},{1... | collective-permute-start | bytes 1572872 | tf_op jit(solution)/shard_map/ppermute | solution.py:22
  52.8 2.9 collective-permute-start.3
  60.4 2.6 collective-permute-start.4
  63.2 14.3 %collective-permute-start.5 = (f32[2,64,1024]{2,1,0:T(8,128)S(1)}, f32[2,64,1024]{2,1,0:T(8,128)S(1)}, u32[]{:S(2)}, u32[]{:S(2)}) collective-permute-start(f32[2,64,1024]{2,1,0:T(8,128)S(1)} %add_select_fusion.7), channel_id=1, source_target_pairs={{0,32},{16,48},{32,0},{48,16},{64,96},{80,112},{96,64},{112,80},{1... | collective-permute-start | bytes 1572872 | tf_op jit(solution)/shard_map/ppermute | solution.py:22
  77.8 17.0 %copy-start.4 = (f32[16]{0:T(128)S(1)}, f32[16]{0:T(128)}, u32[]{:S(2)}) copy-start(f32[16]{0:T(128)} %param.8) | copy-start | bytes 196
  78.1 13.4 %collective-permute-start.6 = (f32[2,64,1024]{2,1,0:T(8,128)S(1)}, f32[2,64,1024]{2,1,0:T(8,128)S(1)}, u32[]{:S(2)}, u32[]{:S(2)}) collective-permute-start(f32[2,64,1024]{2,1,0:T(8,128)S(1)} %add_select_fusion.6), channel_id=1, source_target_pairs={{0,64},{16,80},{32,96},{48,112},{64,0},{80,16},{96,32},{112,48},{1... | collective-permute-start | bytes 1572872 | tf_op jit(solution)/shard_map/ppermute | solution.py:22
  91.8 14.1 %collective-permute-start.7 = (f32[2,64,1024]{2,1,0:T(8,128)S(1)}, f32[2,64,1024]{2,1,0:T(8,128)S(1)}, u32[]{:S(2)}, u32[]{:S(2)}) collective-permute-start(f32[2,64,1024]{2,1,0:T(8,128)S(1)} %add_select_fusion.5), channel_id=1, source_target_pairs={{0,128},{16,144},{32,160},{48,176},{64,192},{80,208},{96,224},{112... | collective-permute-start | bytes 1572872 | tf_op jit(solution)/shard_map/ppermute | solution.py:22
  111.9 371.9 %reduce-scatter.4.cloned.1.call-start = ((), (), s32[]{:S(2)}) async-start(), calls=%async_computation.2 | async-start | bytes 557056
  192.3 7.4 %collective-permute-start.8 = (f32[15,1024]{1,0:T(8,128)S(1)}, f32[15,1024]{1,0:T(8,128)S(1)}, u32[]{:S(2)}, u32[]{:S(2)}) collective-permute-start(f32[15,1024]{1,0:T(8,128)S(1)} %get-tuple-element.54), channel_id=1, source_target_pairs={{0,16},{16,32},{32,48},{48,64},{64,80},{80,96},{96,112},{112,128},... | collective-permute-start | bytes 184328 | tf_op jit(solution)/shard_map/ppermute | solution.py:32
  194.3 6.6 %collective-permute-start.9 = (f32[15,1024]{1,0:T(8,128)S(1)}, f32[15,1024]{1,0:T(8,128)S(1)}, u32[]{:S(2)}, u32[]{:S(2)}) collective-permute-start(f32[15,1024]{1,0:T(8,128)S(1)} %get-tuple-element.55), channel_id=1, source_target_pairs={{16,0},{32,16},{48,32},{64,48},{80,64},{96,80},{112,96},{128,112},... | collective-permute-start | bytes 184328 | tf_op jit(solution)/shard_map/ppermute | solution.py:33
  201.1 20.2 %copy-start.2 = (s32[64,1024]{1,0:T(8,128)S(1)}, s32[64,1024]{1,0:T(8,128)}, u32[]{:S(2)}) copy-start(s32[64,1024]{1,0:T(8,128)} %param.11) | copy-start | bytes 786436
  242.8 7.4 %collective-permute-start.10 = (f32[15,1024]{1,0:T(8,128)S(1)}, f32[15,1024]{1,0:T(8,128)S(1)}, u32[]{:S(2)}, u32[]{:S(2)}) collective-permute-start(f32[15,1024]{1,0:T(8,128)S(1)} %get-tuple-element.52), channel_id=1, source_target_pairs={{0,16},{16,32},{32,48},{48,64},{64,80},{80,96},{96,112},{112,128},... | collective-permute-start | bytes 184328 | tf_op jit(solution)/shard_map/ppermute | solution.py:32
  247.2 4.0 collective-permute-start.11
  297.4 15.7 %collective-permute-start.12 = (f32[2,64,1024]{2,1,0:T(8,128)S(1)}, f32[2,64,1024]{2,1,0:T(8,128)S(1)}, u32[]{:S(2)}, u32[]{:S(2)}) collective-permute-start(f32[2,64,1024]{2,1,0:T(8,128)S(1)} %constant_dynamic-update-slice_fusion.2), channel_id=1, source_target_pairs={{0,128},{16,144},{32,160},{48,176},{64,192},{80,208},{96,224},{112... | collective-permute-start | bytes 1572872 | tf_op jit(solution)/shard_map/ppermute | solution.py:22
  313.4 14.4 %collective-permute-start.13 = (f32[2,64,1024]{2,1,0:T(8,128)S(1)}, f32[2,64,1024]{2,1,0:T(8,128)S(1)}, u32[]{:S(2)}, u32[]{:S(2)}) collective-permute-start(f32[2,64,1024]{2,1,0:T(8,128)S(1)} %maximum_select_fusion.4), channel_id=1, source_target_pairs={{0,64},{16,80},{32,96},{48,112},{64,0},{80,16},{96,32},{112,48},{1... | collective-permute-start | bytes 1572872 | tf_op jit(solution)/shard_map/ppermute | solution.py:22
  328.0 13.5 %collective-permute-start.14 = (f32[2,64,1024]{2,1,0:T(8,128)S(1)}, f32[2,64,1024]{2,1,0:T(8,128)S(1)}, u32[]{:S(2)}, u32[]{:S(2)}) collective-permute-start(f32[2,64,1024]{2,1,0:T(8,128)S(1)} %maximum_select_fusion.5), channel_id=1, source_target_pairs={{0,32},{16,48},{32,0},{48,16},{64,96},{80,112},{96,64},{112,80},{1... | collective-permute-start | bytes 1572872 | tf_op jit(solution)/shard_map/ppermute | solution.py:22
  341.8 2.2 collective-permute-start.15
  348.7 2.0 collective-permute-start.16
  350.9 14.1 %collective-permute-start.17 = (f32[2,64,1024]{2,1,0:T(8,128)S(1)}, f32[2,64,1024]{2,1,0:T(8,128)S(1)}, u32[]{:S(2)}, u32[]{:S(2)}) collective-permute-start(f32[2,64,1024]{2,1,0:T(8,128)S(1)} %add_select_fusion.3), channel_id=1, source_target_pairs={{0,32},{16,48},{32,0},{48,16},{64,96},{80,112},{96,64},{112,80},{1... | collective-permute-start | bytes 1572872 | tf_op jit(solution)/shard_map/ppermute | solution.py:22
  365.5 13.2 %collective-permute-start.18 = (f32[2,64,1024]{2,1,0:T(8,128)S(1)}, f32[2,64,1024]{2,1,0:T(8,128)S(1)}, u32[]{:S(2)}, u32[]{:S(2)}) collective-permute-start(f32[2,64,1024]{2,1,0:T(8,128)S(1)} %add_select_fusion.2), channel_id=1, source_target_pairs={{0,64},{16,80},{32,96},{48,112},{64,0},{80,16},{96,32},{112,48},{1... | collective-permute-start | bytes 1572872 | tf_op jit(solution)/shard_map/ppermute | solution.py:22
  379.0 13.8 %collective-permute-start.19 = (f32[2,64,1024]{2,1,0:T(8,128)S(1)}, f32[2,64,1024]{2,1,0:T(8,128)S(1)}, u32[]{:S(2)}, u32[]{:S(2)}) collective-permute-start(f32[2,64,1024]{2,1,0:T(8,128)S(1)} %add_select_fusion.1), channel_id=1, source_target_pairs={{0,128},{16,144},{32,160},{48,176},{64,192},{80,208},{96,224},{112... | collective-permute-start | bytes 1572872 | tf_op jit(solution)/shard_map/ppermute | solution.py:22
  (3 other events, 34.9 us)
Sparse Core Ops, SparseCore 0:
  112.1 77.7 all-gather.1
  397.7 86.0 reduce-scatter.3
